TPU v7x, 32 devices: a whole 2x2x4 slice. The times are simulated.
32 devices in a mesh: row: 8 (over z, y), col: 4 (over x, core).
Axes of the slice: x: 2, y: 2, z: 4, core: 2. Of those that a mesh axis runs over, the one named last changes fastest.
Arguments:
- nodes_zero: float32 [8192, 64], P('row'), may hold values from -28 to 28
- nodes_one: float32 [8192, 64], P(('row', 'col')), may hold values from -28 to 28
- nodes_two: float32 [8192, 64], P('col'), may hold values from -28 to 28
- precision: float32 [64], replicated, may hold values from 0.1 to 0.4
- drift: float32 [64], replicated, may hold values from -1.2 to 1.2
- terminal: bfloat16 [8192, 128], P('col'), may hold values from -6 to 6
- exercise_one: float32 [8192, 128], P(('row', 'col')), may hold values from -6 to 6
- exercise_zero: float32 [8192, 128], P(('row', 'col')), may hold values from -6 to 6
- exercise_flags: int32 [2, 128], replicated, may hold values 0 or 1
Outputs:
- value_one: float32 [8192, 128], P(('row', 'col'))
- value_zero: float32 [8192, 128], P(('row', 'col'))
All inputs are finite; a program needn't handle non-finite values.
Results may differ from a plain program's by a relative error of at most 0.0012.
Values may be sent and summed in bfloat16 or wider, within the bound.
A program may use at most 64 MiB of HBM per device.

v0:
```python
import jax
import jax.numpy as jnp
from jax import lax
from jax.sharding import PartitionSpec as P


def pair_scores(queries, offsets, targets):
    product = lax.dot_general(
        queries, targets, (((1,), (1,)), ((), ())), preferred_element_type=jnp.float32
    )
    return product - offsets[:, None]


def continuation(sources, targets, prices, precision, drift):
    shifted = sources + drift
    queries = (shifted * precision).astype(jnp.bfloat16)
    offsets = 0.5 * jnp.sum(precision * shifted * shifted, axis=1)
    target_count = targets.shape[0]
    block_width = min(512, target_count)
    blocks = target_count // block_width
    target_blocks = targets.reshape(blocks, block_width, targets.shape[1])
    price_blocks = prices.reshape(blocks, block_width, prices.shape[1])

    def local_stats(target_block):
        scores = pair_scores(queries, offsets, target_block)
        column_peak = jnp.max(scores, axis=0)
        return (column_peak, jnp.sum(jnp.exp(scores - column_peak[None, :]), axis=0))

    maxima, totals = lax.map(local_stats, target_blocks)
    highest = lax.pmax(maxima, "row")
    totals = lax.psum(totals * jnp.exp(maxima - highest), "row")
    maxima = highest
    inverse = 1.0 / totals
    share_rows = sources.shape[0] // lax.axis_size("col")

    def accumulate(running, pieces):
        target_block, column_peak, column_inverse, price_block = pieces
        scores = pair_scores(queries, offsets, target_block)
        weights = (jnp.exp(scores - column_peak[None, :]) * column_inverse[None, :]).astype(
            jnp.bfloat16
        )
        return (running + jnp.dot(weights, price_block, preferred_element_type=jnp.float32), None)

    start = jnp.zeros((share_rows * lax.axis_size("col"), prices.shape[1]), jnp.float32)
    running, unused = lax.scan(accumulate, start, (target_blocks, maxima, inverse, price_blocks))
    return lax.psum_scatter(running, "col", scatter_dimension=0, tiled=True)


def settle(carried, exercise, allowed):
    return jnp.where(allowed[None, :] == 1, jnp.maximum(exercise, carried), carried)


def shards(
    nodes_zero,
    nodes_one,
    nodes_two,
    precision,
    drift,
    terminal,
    exercise_one,
    exercise_zero,
    exercise_flags,
):
    sources = lax.all_gather(nodes_one, "col", axis=0, tiled=True)
    carry_one = continuation(sources, nodes_two.astype(jnp.bfloat16), terminal, precision, drift)
    value_one = settle(carry_one, exercise_one, exercise_flags[1])
    target_one, price_one = (
        lax.all_gather(nodes_one.astype(jnp.bfloat16), "row", axis=0, tiled=True),
        lax.all_gather(value_one.astype(jnp.bfloat16), "row", axis=0, tiled=True),
    )
    carry_zero = continuation(nodes_zero, target_one, price_one, precision, drift)
    value_zero = settle(carry_zero, exercise_zero, exercise_flags[0])
    return (value_one, value_zero)


def solution(mesh):
    placed = (
        P("row", None),
        P(("row", "col"), None),
        P("col", None),
        P(),
        P(),
        P("col", None),
        P(("row", "col"), None),
        P(("row", "col"), None),
        P(),
    )
    return jax.shard_map(
        shards,
        mesh=mesh,
        in_specs=placed,
        out_specs=(P(("row", "col"), None), P(("row", "col"), None)),
        check_vma=False,
    )
```

profile of v0, /device:TPU:1, one launch (start us, length us, event | category | flops | bytes accessed | tf_op | source)
XLA Modules:
  0.0 226.2 jit_solution(406168056470124395)
XLA Ops:
  7.2 0.0 reduce-scatter.3.cloned.1.call-start
  7.2 0.9 copy.12
  8.1 0.8 convert_element_type.19
  9.0 8.5 %all_gather.9 = f32[1024,64]{1,0:T(8,128)S(1)} all-gather(f32[256,64]{1,0:T(8,128)S(1)} %copy.12), channel_id=1, replica_groups=mesh['row'=8,'col'=4] {'col'}, dimensions={0}, use_global_device_ids=true | all-gather | bytes 327680 | tf_op jit(solution)/shard_map/all_gather | solution.py:64
  17.5 1.1 copy.14
  18.6 1.0 fusion.35
  19.7 24.7 %all_gather.10 = bf16[2048,64]{0,1:T(8,128)(2,1)S(1)} all-gather(bf16[256,64]{0,1:T(8,128)(2,1)S(1)} %convert_element_type.19), channel_id=1, replica_groups=mesh['row'=8,'col'=4] {'row'}, dimensions={0}, use_global_device_ids=true | all-gather | bytes 294912 | tf_op jit(solution)/shard_map/all_gather | solution.py:68
  44.4 0.3 copy.13
  44.7 0.0 copy-start
  44.7 4.7 %while.47 = (s32[]{:T(128)}, f32[4,512]{1,0:T(4,128)S(1)}, f32[4,512]{1,0:T(4,128)S(1)}, bf16[4,512,64]{2,1,0:T(8,128)(2,1)S(1)}, bf16[1024,64]{1,0:T(8,128)(2,1...) while((s32[]{:T(128)}, f32[4,512]{1,0:T(4,128)S(1)}, f32[4,512]{1,0:T(4,128)S(1)}, ...), condition=%wide.region_14.15_spmd, body=%wide.region_11.14_spmd.sunk | while | flops 69729280 | bytes 4610145 | solution.py:29
  44.7 0.5 subtract_reduce_fusion.5
  45.2 0.5 exponential_reduce_fusion.5
  45.8 0.1 dynamic_update_slice.19
  45.9 0.5 subtract_reduce_fusion.5
  46.4 0.5 exponential_reduce_fusion.5
  47.0 0.1 dynamic_update_slice.19
  47.1 0.5 subtract_reduce_fusion.5
  47.6 0.5 exponential_reduce_fusion.5
  48.2 0.1 dynamic_update_slice.19
  48.2 0.5 subtract_reduce_fusion.5
  48.8 0.5 exponential_reduce_fusion.5
  49.3 0.1 dynamic_update_slice.19
  49.4 0.0 copy-done
  49.5 0.3 copy.11
  49.8 4.7 %while.46 = (s32[]{:T(128)}, f32[4,512]{1,0:T(4,128)S(1)}, f32[4,512]{1,0:T(4,128)S(1)}, bf16[4,512,64]{2,1,0:T(8,128)(2,1)S(1)}, bf16[1024,64]{1,0:T(8,128)(2,1...) while((s32[]{:T(128)}, f32[4,512]{1,0:T(4,128)S(1)}, f32[4,512]{1,0:T(4,128)S(1)}, ...), condition=%wide.region_4.5_spmd, body=%wide.region_1.4_spmd.sunk | while | flops 69729280 | bytes 4610145 | solution.py:29
  49.8 0.5 subtract_reduce_fusion.4
  50.3 0.5 exponential_reduce_fusion.4
  50.9 0.1 dynamic_update_slice.17
  51.0 0.5 subtract_reduce_fusion.4
  51.5 0.5 exponential_reduce_fusion.4
  52.1 0.1 dynamic_update_slice.17
  52.1 0.5 subtract_reduce_fusion.4
  52.7 0.5 exponential_reduce_fusion.4
  53.3 0.1 dynamic_update_slice.17
  53.3 0.5 subtract_reduce_fusion.4
  53.8 0.5 exponential_reduce_fusion.4
  54.4 0.1 dynamic_update_slice.17
  54.5 30.2 %all-reduce.1 = (f32[4,512]{1,0:T(4,128)S(1)}, f32[4,512]{1,0:T(4,128)S(1)}) all-reduce(f32[4,512]{1,0:T(4,128)S(1)} %get-tuple-element.152, f32[4,512]{1,0:T(4,128)S(1)} %get-tuple-element.155), channel_id=1, replica_groups=mesh['row'=8,'col'=4] {'row'}, use_global_device_ids=true, to_apply=%region_5.6 | all-reduce | flops 4096 | bytes 32768 | tf_op jit(solution)/shard_map/pmax | solution.py:30
  84.7 26.0 %all-reduce = (f32[4,512]{1,0:T(4,128)S(1)}, f32[4,512]{1,0:T(4,128)S(1)}) all-reduce(f32[4,512]{1,0:T(4,128)S(1)} %get-tuple-element.289, f32[4,512]{1,0:T(4,128)S(1)} %get-tuple-element.288), channel_id=1, replica_groups=mesh['row'=8,'col'=4] {'row'}, use_global_device_ids=true, to_apply=%region_6.7 | all-reduce | flops 4096 | bytes 32768 | tf_op jit(solution)/shard_map/psum | solution.py:31
  110.8 0.0 copy-start.4
  110.8 8.0 %while.48 = (s32[]{:T(128)}, f32[1024,128]{1,0:T(8,128)S(1)}, bf16[4,512,64]{2,1,0:T(8,128)(2,1)S(1)}, bf16[1024,64]{1,0:T(8,128)(2,1)S(1)}, f32[1024]{0:T(1024)...) while((s32[]{:T(128)}, f32[1024,128]{1,0:T(8,128)S(1)}, ...), condition=%wide.region_8.9_spmd.clone, body=%wide.region_7.8_spmd.clone.sunk | while | flops 203685888 | bytes 1590387 | solution.py:45
  110.8 2.0 fusion.56
  112.9 1.9 fusion.56
  114.9 1.9 fusion.56
  116.8 1.9 fusion.56
  118.8 0.0 copy-start.1
  118.8 0.8 copy-done.1
  119.6 0.0 reduce-scatter.3.cloned.1.call-update
  119.6 0.0 reduce-scatter.5.cloned.1.call-start
  119.7 0.0 copy-done.5
  119.7 38.0 %reduce-scatter.3.cloned.1.call-done = f32[256,128]{1,0:T(8,128)} async-done(((f32[1024,128]{1,0:T(8,128)}), f32[256,128]{1,0:T(8,128)}) %reduce-scatter.3.cloned.1.call-update) | async-done | bytes 131088 | tf_op jit(solution)/shard_map/reduce_scatter | solution.py:46
  157.7 0.0 copy-done.4
  157.8 1.6 fusion.36
  159.3 25.9 %all_gather.11 = bf16[2048,128]{1,0:T(8,128)(2,1)S(1)} all-gather(bf16[256,128]{1,0:T(8,128)(2,1)S(1)} %get-tuple-element.274), channel_id=1, replica_groups=mesh['row'=8,'col'=4] {'row'}, dimensions={0}, use_global_device_ids=true | all-gather | bytes 589824 | tf_op jit(solution)/shard_map/all_gather | solution.py:69
  185.3 4.3 %while.49 = (s32[]{:T(128)}, f32[1024,128]{1,0:T(8,128)S(1)}, bf16[4,512,64]{2,1,0:T(8,128)(2,1)S(1)}, bf16[1024,64]{1,0:T(8,128)(2,1)S(1)}, f32[1024]{0:T(1024)...) while((s32[]{:T(128)}, f32[1024,128]{1,0:T(8,128)S(1)}, ...), condition=%wide.region_18.19_spmd.clone, body=%wide.region_17.18_spmd.clone.sunk | while | flops 203685888 | bytes 1590387 | solution.py:45
  185.3 1.0 fusion.60
  186.4 1.0 fusion.60
  187.4 1.0 fusion.60
  188.5 1.0 fusion.60
  189.6 0.8 copy-done.2
  190.3 0.0 reduce-scatter.5.cloned.1.call-update
  190.4 27.4 %reduce-scatter.5.cloned.1.call-done = f32[256,128]{1,0:T(8,128)} async-done(((f32[1024,128]{1,0:T(8,128)}), f32[256,128]{1,0:T(8,128)}) %reduce-scatter.5.cloned.1.call-update) | async-done | bytes 131088 | tf_op jit(solution)/shard_map/reduce_scatter | solution.py:46
  217.8 0.0 copy-done.3
  217.8 1.6 maximum_select_fusion
  (32 shorter events, 0.5 us)
Async XLA Ops:
  7.2 150.6 %reduce-scatter.3.cloned.1.call-start = ((), (), s32[]{:S(2)}) async-start(), calls=%async_computation.2 | async-start | bytes 655360 | tf_op jit(solution)/shard_map/reduce_scatter | solution.py:46
  44.7 4.7 %copy-start = (f32[2048,64]{0,1:T(8,128)S(1)}, f32[2048,64]{0,1:T(8,128)}, u32[]{:S(2)}) copy-start(f32[2048,64]{0,1:T(8,128)} %param.19) | copy-start | bytes 1572868
  110.8 8.9 %copy-start.5 = (s32[2,128]{1,0:T(2,128)S(1)}, s32[2,128]{1,0:T(2,128)}, u32[]{:S(2)}) copy-start(s32[2,128]{1,0:T(2,128)} %param.25) | copy-start | bytes 3076
  110.8 47.0 %copy-start.4 = (f32[256,128]{1,0:T(8,128)S(1)}, f32[256,128]{1,0:T(8,128)}, u32[]{:S(2)}) copy-start(f32[256,128]{1,0:T(8,128)} %param.23) | copy-start | bytes 393220
  118.8 0.8 copy-start.1
  119.6 98.2 %reduce-scatter.5.cloned.1.call-start = ((), (), s32[]{:S(2)}) async-start(), calls=%async_computation.3 | async-start | bytes 655360 | tf_op jit(solution)/shard_map/reduce_scatter | solution.py:46
  185.3 32.5 %copy-start.3 = (f32[256,128]{1,0:T(8,128)S(1)}, f32[256,128]{1,0:T(8,128)}, u32[]{:S(2)}) copy-start(f32[256,128]{1,0:T(8,128)} %param.24) | copy-start | bytes 393220
  189.5 0.8 copy-start.2
Sparse Core Ops, SparseCore 0:
  119.7 37.9 reduce-scatter.2
  190.5 27.2 reduce-scatter.4
where the time goes:
time: 227 us; the launch traced here: 226 us
  blocking collectives  115 us (51%)
  waiting for transfers between devices  65.5 us (29%)
  matrix products  16.1 us (7%)
  between operations  14.2 us (6%)
  other arithmetic  9.42 us (4%)
  local copies, waits for them, and re-layouts  5.05 us (2%)
    reduce_scatter x2, waiting for transfers between devices, continuation(): return lax.psum_scatter(running, 'col', scatter_dimension=0, tiled=True)  65.4 us
    pmax x1, blocking collectives, continuation(): highest = lax.pmax(maxima, 'row')  30.2 us
    psum x1, blocking collectives, continuation(): totals = lax.psum(totals * jnp.exp(maxima - highest), 'row')  26 us
    all_gather x1, blocking collectives, shards(): lax.all_gather(value_one.astype(jnp.bfloat16), 'row', axis=0, tiled=True)  25.9 us
    all_gather x1, blocking collectives, shards(): lax.all_gather(nodes_one.astype(jnp.bfloat16), 'row', axis=0, tiled=True)  24.7 us
    dot_general x8, matrix products, accumulate(): jnp.dot(weights, price_block, preferred_element_type=jnp.float32)  11.9 us
    all_gather x1, blocking collectives, shards(): sources = lax.all_gather(nodes_one, 'col', axis=0, tiled=True)  8.49 us
  transfers between devices with their start and end apart: 2, of which 2 were waited for; matrix products, arithmetic and copies ran while one was open for 0% of the time, Pallas kernels for 0%

commit v1 on v0

v1 whole, which is shorter than its diff:
```python
import functools

import jax
import jax.numpy as jnp
from jax import lax
from jax.experimental import pallas as pl
from jax.experimental.pallas import tpu as pltpu
from jax.sharding import PartitionSpec as P

MESH = pl.DeviceIdType.MESH
TILE = 256


def pieces_of(column, lanes):
    first = column.astype(jnp.bfloat16).astype(jnp.float32)
    rest = column - first
    second = rest.astype(jnp.bfloat16).astype(jnp.float32)
    third = rest - second
    lane = lax.broadcasted_iota(jnp.int32, (column.shape[0], lanes), 1)
    out = jnp.where(lane == 0, first, jnp.where(lane == 1, second, jnp.where(lane == 2, third, 0.0)))
    return out.astype(jnp.bfloat16)


def put_queries(view, nodes, precision, drift):
    depth = nodes.shape[1]
    shifted = nodes + drift
    view[:, :depth] = (shifted * precision).astype(jnp.bfloat16)
    offsets = 0.5 * jnp.sum(precision * shifted * shifted, axis=1, keepdims=True)
    view[:, depth:] = pieces_of(offsets, view.shape[1] - depth)


def put_targets(view, nodes):
    depth = nodes.shape[1]
    view[:, :depth] = nodes.astype(jnp.bfloat16)
    lane = lax.broadcasted_iota(jnp.int32, (nodes.shape[0], view.shape[1] - depth), 1)
    view[:, depth:] = jnp.where(lane < 3, -1.0, 0.0).astype(jnp.bfloat16)


def body(
    rows,
    cols,
    nz_ref,
    n1_ref,
    n2_ref,
    precision_ref,
    drift_ref,
    terminal_ref,
    ex1_ref,
    ex0_ref,
    flags_ref,
    v1_ref,
    v0_ref,
    q1,
    t1,
    q0,
    t2,
    e1,
    e0,
    st1,
    st0,
    f1,
    f0,
    price,
    out1,
    in1,
    out0,
    in0,
    q_send,
    q_recv,
    t_send,
    t_recv,
    s1_send,
    s1_recv,
    s0_send,
    s0_recv,
    p_send,
    p_recv,
    r1_send,
    r1_recv,
    r0_send,
    r0_recv,
):
    r = lax.axis_index("row")
    c = lax.axis_index("col")
    own = n1_ref.shape[0]
    sources = nz_ref.shape[0]
    targets = n2_ref.shape[0]
    chunks, _, width = e1.shape
    precision = precision_ref[...]
    drift = drift_ref[...]

    barrier = pltpu.get_barrier_semaphore()
    for d in range(1, rows):
        pl.semaphore_signal(barrier, inc=1, device_id=(lax.rem(r + d, rows), c), device_id_type=MESH)
    for d in range(1, cols):
        pl.semaphore_signal(barrier, inc=1, device_id=(r, lax.rem(c + d, cols)), device_id_type=MESH)

    put_queries(q1.at[c], n1_ref[...], precision, drift)
    put_targets(t1.at[r], n1_ref[...])
    pl.semaphore_wait(barrier, rows + cols - 2)

    def to_rows(buf, send, recv):
        def make(d, slot):
            return pltpu.make_async_remote_copy(
                src_ref=buf.at[slot],
                dst_ref=buf.at[slot],
                send_sem=send.at[d],
                recv_sem=recv.at[d],
                device_id=(lax.rem(r + d, rows), c),
                device_id_type=MESH,
            )

        return make

    def start_rows(buf, send, recv):
        make = to_rows(buf, send, recv)
        for d in range(1, rows):
            make(d, r).start()

    def recv_rows(buf, send, recv):
        make = to_rows(buf, send, recv)
        for d in range(1, rows):
            make(d, lax.rem(r + rows - d, rows)).wait_recv()

    def sent_rows(buf, send, recv):
        make = to_rows(buf, send, recv)
        for d in range(1, rows):
            make(d, r).wait_send()

    def q_copy(d, slot):
        return pltpu.make_async_remote_copy(
            src_ref=q1.at[slot],
            dst_ref=q1.at[slot],
            send_sem=q_send.at[d],
            recv_sem=q_recv.at[d],
            device_id=(r, lax.rem(c + d, cols)),
            device_id_type=MESH,
        )

    for d in range(1, cols):
        q_copy(d, c).start()
    start_rows(t1, t_send, t_recv)

    put_targets(t2, n2_ref[...])
    put_queries(q0, nz_ref[...], precision, drift)

    step = min(TILE, sources)

    def stats(load_queries, load_targets, e, st, slot):
        def one(k, carry):
            target = load_targets(k)
            peak = None
            for at in range(0, sources, step):
                s = lax.dot_general(
                    load_queries(at), target, (((1,), (1,)), ((), ())), preferred_element_type=jnp.float32
                )
                e[k, at : at + step, :] = s
                top = jnp.max(s.reshape(step // 8, 8, width), axis=0)
                peak = top if peak is None else jnp.maximum(peak, top)
            peak = jnp.max(peak, axis=0, keepdims=True)
            total = jnp.zeros((8, width), jnp.float32)
            for at in range(0, sources, step):
                x = jnp.exp(e[k, at : at + step, :] - peak)
                e[k, at : at + step, :] = x
                total = total + jnp.sum(x.reshape(step // 8, 8, width), axis=0)
            st[slot, 0, pl.ds(k, 1), :] = peak
            st[slot, 1, pl.ds(k, 1), :] = jnp.sum(total, axis=0, keepdims=True)
            return carry

        lax.fori_loop(0, chunks, one, 0)

    def factor(st, f):
        peak = st[0, 0]
        for i in range(1, rows):
            peak = jnp.maximum(peak, st[i, 0])
        total = jnp.zeros_like(peak)
        for i in range(rows):
            total = total + st[i, 1] * jnp.exp(st[i, 0] - peak)
        f[...] = jnp.exp(st[r, 0] - peak) * (1.0 / total)

    for d in range(1, cols):
        q_copy(d, lax.rem(c + cols - d, cols)).wait_recv()

    def q1_rows(at):
        return q1[at // own : (at + step) // own].reshape(step, q1.shape[2])

    stats(q1_rows, lambda k: t2[pl.ds(k * width, width), :], e1, st1, r)
    start_rows(st1, s1_send, s1_recv)

    recv_rows(t1, t_send, t_recv)
    per = width // own

    def t1_rows(k):
        return t1[pl.ds(k * per, per)].reshape(width, t1.shape[2])

    stats(lambda at: q0[at : at + step, :], t1_rows, e0, st0, r)
    start_rows(st0, s0_send, s0_recv)

    recv_rows(st1, s1_send, s1_recv)
    factor(st1, f1)

    def partial_of(e, f, load_prices, block):
        def one(k, total):
            w = (e[k, pl.ds(block * own, own), :] * f[pl.ds(k, 1), :]).astype(jnp.bfloat16)
            return total + jnp.dot(w, load_prices(k), preferred_element_type=jnp.float32)

        return lax.fori_loop(0, chunks, one, jnp.zeros((own, v1_ref.shape[1]), jnp.float32))

    def reduce(e, f, load_prices, out, into, send, recv):
        def make(d):
            return pltpu.make_async_remote_copy(
                src_ref=out.at[d],
                dst_ref=into.at[d],
                send_sem=send.at[d],
                recv_sem=recv.at[d],
                device_id=(r, lax.rem(c + d, cols)),
                device_id_type=MESH,
            )

        for d in range(1, cols):
            out[d] = partial_of(e, f, load_prices, lax.rem(c + d, cols))
            make(d).start()
        total = partial_of(e, f, load_prices, c)
        for d in range(1, cols):
            make(d).wait_recv()
            total = total + into[d]
        return total, lambda: [make(d).wait_send() for d in range(1, cols)]

    carried, done1 = reduce(
        e1, f1, lambda k: terminal_ref[pl.ds(k * width, width), :], out1, in1, r1_send, r1_recv
    )
    value = jnp.where(flags_ref[1:2, :] == 1, jnp.maximum(ex1_ref[...], carried), carried)
    v1_ref[...] = value
    price[r] = value.astype(jnp.bfloat16)
    start_rows(price, p_send, p_recv)

    recv_rows(st0, s0_send, s0_recv)
    factor(st0, f0)
    recv_rows(price, p_send, p_recv)

    def price_rows(k):
        return price[pl.ds(k * per, per)].reshape(width, price.shape[2])

    carried, done0 = reduce(e0, f0, price_rows, out0, in0, r0_send, r0_recv)
    v0_ref[...] = jnp.where(flags_ref[0:1, :] == 1, jnp.maximum(ex0_ref[...], carried), carried)

    for d in range(1, cols):
        q_copy(d, c).wait_send()
    sent_rows(t1, t_send, t_recv)
    sent_rows(st1, s1_send, s1_recv)
    sent_rows(st0, s0_send, s0_recv)
    sent_rows(price, p_send, p_recv)
    done1()
    done0()


def shards(rows, cols, nodes_zero, nodes_one, nodes_two, precision, drift, terminal, ex1, ex0, flags):
    own, depth = nodes_one.shape
    sources = nodes_zero.shape[0]
    targets = nodes_two.shape[0]
    trades = terminal.shape[1]
    width = max(own, min(TILE, targets))
    chunks = targets // width
    lanes = 128 * (-(-(depth + 3) // 128))
    dma = pltpu.SemaphoreType.DMA
    vmem = pl.BlockSpec(memory_space=pltpu.VMEM)
    out = jax.ShapeDtypeStruct((own, trades), jnp.float32)
    stat = pltpu.VMEM((rows, 2, chunks, width), jnp.float32)
    tall = pltpu.VMEM((chunks, sources, width), jnp.float32)
    few = pltpu.VMEM((chunks, width), jnp.float32)
    parts = pltpu.VMEM((cols, own, trades), jnp.float32)
    return pl.pallas_call(
        functools.partial(body, rows, cols),
        out_shape=(out, out),
        in_specs=[vmem] * 9,
        out_specs=(vmem, vmem),
        scratch_shapes=[
            pltpu.VMEM((cols, own, lanes), jnp.bfloat16),
            pltpu.VMEM((rows, own, lanes), jnp.bfloat16),
            pltpu.VMEM((sources, lanes), jnp.bfloat16),
            pltpu.VMEM((targets, lanes), jnp.bfloat16),
            tall,
            tall,
            stat,
            stat,
            few,
            few,
            pltpu.VMEM((rows, own, trades), jnp.bfloat16),
            parts,
            parts,
            parts,
            parts,
            dma((cols,)),
            dma((cols,)),
            dma((rows,)),
            dma((rows,)),
            dma((rows,)),
            dma((rows,)),
            dma((rows,)),
            dma((rows,)),
            dma((rows,)),
            dma((rows,)),
            dma((cols,)),
            dma((cols,)),
            dma((cols,)),
            dma((cols,)),
        ],
        compiler_params=pltpu.CompilerParams(
            collective_id=0, has_side_effects=True, vmem_limit_bytes=56 * 1024 * 1024
        ),
    )(nodes_zero, nodes_one, nodes_two, precision[None, :], drift[None, :], terminal, ex1, ex0, flags)


def solution(mesh):
    both = P(("row", "col"), None)
    return jax.shard_map(
        functools.partial(shards, mesh.shape["row"], mesh.shape["col"]),
        mesh=mesh,
        in_specs=(P("row", None), both, P("col", None), P(), P(), P("col", None), both, both, P()),
        out_specs=(both, both),
        check_vma=False,
    )
```

time: 227 us -> 61.9 us (0.27)
  the two profiles are of different devices: /device:TPU:1 before, /device:TPU:25 now
where the time goes in v1:
time: 61.9 us; the launch traced here: 61.6 us
  Pallas kernels  53.8 us (87%)
  local copies, waits for them, and re-layouts  7.18 us (12%)
  between operations  0.66 us (1%)
    pallas_call x1, Pallas kernels, shards(): pl.pallas_call(functools.partial(body, rows, cols), out_shape=(out, out),...  53.8 us
    unnamed x9, local copies, waits for them, and re-layouts  7.18 us

profile of v1, /device:TPU:25, one launch (start us, length us, event | category | flops | bytes accessed | tf_op | source)
XLA Modules:
  0.0 61.6 jit_solution(5936672029970118563)
XLA Ops:
  0.6 0.0 copy-start
  0.6 1.7 %copy.12.n1_ref = f32[256,64]{1,0:T(8,128)} copy(f32[256,64]{0,1:T(8,128)} %param.10) | data formatting | bytes 131072 | tf_op args[1]
  2.3 2.0 %copy.11.nz_ref = f32[1024,64]{1,0:T(8,128)} copy(f32[1024,64]{0,1:T(8,128)} %param.9) | data formatting | bytes 524288 | tf_op args[0]
  4.2 0.0 copy-done
  4.2 1.3 %copy.13.n2_ref = f32[2048,64]{1,0:T(8,128)} copy(f32[2048,64]{0,1:T(8,128)S(1)} %copy-done) | data formatting | bytes 1048576 | tf_op args[2]
  5.6 53.8 %shard_map.104 = (f32[256,128]{1,0:T(8,128)}, f32[256,128]{1,0:T(8,128)}) custom-call(f32[1024,64]{1,0:T(8,128)} %copy.11.nz_ref, f32[256,64]{1,0:T(8,128)} %copy.12.n1_ref, f32[2048,64]{1,0:T(8,128)} %copy.13.n2_ref, f32[1,64]{1,0:T(1,128)} %bitcast.2, f32[1,64]{1,0:T(1,128)} %bitcast.3, bf16[2048,128]{1,0:T(8,128)(2,1)} %terminal_ref.1, ...), custom_call_target="tpu_custom_call" | custom-call | tf_op jit(solution)/shard_map/pallas_call | solution.py:272
  59.4 0.0 copy-start.1
  59.4 1.6 %copy.16 = f32[256,128]{1,0:T(8,128)} copy(f32[256,128]{1,0:T(8,128)} %get-tuple-element.4) | data formatting | bytes 262144
  61.0 0.0 copy-done.1
  61.0 0.7 %copy.17 = f32[256,128]{1,0:T(8,128)} copy(f32[256,128]{1,0:T(8,128)S(1)} %copy-done.1) | data formatting | bytes 262144
Async XLA Ops:
  0.6 3.6 %copy-start = (f32[2048,64]{0,1:T(8,128)S(1)}, f32[2048,64]{0,1:T(8,128)}, u32[]{:S(2)}) copy-start(f32[2048,64]{0,1:T(8,128)} %param.11) | copy-start | bytes 1572868
  59.4 1.6 %copy-start.1 = (f32[256,128]{1,0:T(8,128)S(1)}, f32[256,128]{1,0:T(8,128)}, u32[]{:S(2)}) copy-start(f32[256,128]{1,0:T(8,128)} %get-tuple-element.5) | copy-start | bytes 393220

commit v2 on v1

v2 whole, which is shorter than its diff:
```python
import functools

import jax
import jax.numpy as jnp
from jax import lax
from jax.experimental import pallas as pl
from jax.experimental.pallas import tpu as pltpu
from jax.sharding import PartitionSpec as P

MESH = pl.DeviceIdType.MESH
TILE = 256


def column_of(row):
    return jnp.broadcast_to(row, (128, row.shape[1])).T[:, :1]


def queries_of(nodes, precision, drift, height):
    shifted = nodes + drift
    offsets = 0.5 * jnp.sum(precision * shifted * shifted, axis=0, keepdims=True)
    first = offsets.astype(jnp.bfloat16).astype(jnp.float32)
    rest = offsets - first
    second = rest.astype(jnp.bfloat16).astype(jnp.float32)
    third = rest - second
    count = height - nodes.shape[0]
    at = lax.broadcasted_iota(jnp.int32, (count, nodes.shape[1]), 0)
    extra = jnp.where(at == 0, first, jnp.where(at == 1, second, jnp.where(at == 2, third, 0.0)))
    return jnp.concatenate([shifted * precision, extra], axis=0)


def upright(tall, lanes):
    short = lanes - tall.shape[0]
    if short:
        tall = jnp.concatenate([tall, jnp.zeros((short, tall.shape[1]), tall.dtype)], axis=0)
    return tall.T.astype(jnp.bfloat16)


def ones_under(count, width):
    at = lax.broadcasted_iota(jnp.int32, (count, width), 0)
    return jnp.where(at < 3, -1.0, 0.0).astype(jnp.bfloat16)


def body(
    rows,
    cols,
    nz_ref,
    n1_ref,
    n2_ref,
    precision_ref,
    drift_ref,
    terminal_ref,
    ex1_ref,
    ex0_ref,
    flags_ref,
    v1_ref,
    v0_ref,
    q1t,
    q1,
    t1,
    q0,
    t2,
    e1,
    e0,
    w0,
    st1,
    st0,
    f1,
    f0,
    price,
    out1,
    in1,
    out0,
    in0,
    q_send,
    q_recv,
    t_send,
    t_recv,
    s1_send,
    s1_recv,
    s0_send,
    s0_recv,
    p_send,
    p_recv,
    r1_send,
    r1_recv,
    r0_send,
    r0_recv,
):
    r = lax.axis_index("row")
    c = lax.axis_index("col")
    depth, own = n1_ref.shape
    sources = nz_ref.shape[1]
    lanes = q0.shape[1]
    height = q1t.shape[1]
    chunks, _, width = e1.shape
    precision = column_of(precision_ref[...])
    drift = column_of(drift_ref[...])

    barrier = pltpu.get_barrier_semaphore()
    for d in range(1, rows):
        pl.semaphore_signal(barrier, inc=1, device_id=(lax.rem(r + d, rows), c), device_id_type=MESH)
    for d in range(1, cols):
        pl.semaphore_signal(barrier, inc=1, device_id=(r, lax.rem(c + d, cols)), device_id_type=MESH)

    mine = queries_of(n1_ref[...], precision, drift, height)
    q1t[c] = mine.astype(jnp.bfloat16)
    t1[r, :depth, :] = n1_ref[...].astype(jnp.bfloat16)
    pl.semaphore_wait(barrier, rows + cols - 2)

    def to_rows(buf, send, recv):
        def make(d, slot):
            view = buf.at[slot, pl.ds(0, depth)] if buf is t1 else buf.at[slot]
            return pltpu.make_async_remote_copy(
                src_ref=view,
                dst_ref=view,
                send_sem=send.at[d],
                recv_sem=recv.at[d],
                device_id=(lax.rem(r + d, rows), c),
                device_id_type=MESH,
            )

        return make

    def start_rows(buf, send, recv):
        make = to_rows(buf, send, recv)
        for d in range(1, rows):
            make(d, r).start()

    def recv_rows(buf, send, recv):
        make = to_rows(buf, send, recv)
        for d in range(1, rows):
            make(d, lax.rem(r + rows - d, rows)).wait_recv()

    def sent_rows(buf, send, recv):
        make = to_rows(buf, send, recv)
        for d in range(1, rows):
            make(d, r).wait_send()

    def q_copy(d, slot):
        return pltpu.make_async_remote_copy(
            src_ref=q1t.at[slot],
            dst_ref=q1t.at[slot],
            send_sem=q_send.at[d],
            recv_sem=q_recv.at[d],
            device_id=(r, lax.rem(c + d, cols)),
            device_id_type=MESH,
        )

    for d in range(1, cols):
        q_copy(d, c).start()
    start_rows(t1, t_send, t_recv)

    for k in range(chunks):
        t2[k, :depth, :] = n2_ref[:, k * width : (k + 1) * width].astype(jnp.bfloat16)
        t2[k, depth:, :] = ones_under(lanes - depth, width)
    q1[c] = upright(mine, lanes)
    q0[...] = upright(queries_of(nz_ref[...], precision, drift, height), lanes)
    for i in range(rows):
        t1[i, depth:, :] = ones_under(lanes - depth, own)

    step = min(TILE, sources)

    def stats(load_queries, load_targets, e, st, begin, end):
        def one(k, carry):
            target = load_targets(k)
            peak = None
            for at in range(0, sources, step):
                s = lax.dot_general(
                    load_queries(at), target, (((1,), (0,)), ((), ())), preferred_element_type=jnp.float32
                )
                e[k, at : at + step, :] = s
                top = jnp.max(s.reshape(step // 8, 8, width), axis=0)
                peak = top if peak is None else jnp.maximum(peak, top)
            peak = jnp.max(peak, axis=0, keepdims=True)
            total = jnp.zeros((8, width), jnp.float32)
            for at in range(0, sources, step):
                x = jnp.exp(e[k, at : at + step, :] - peak)
                e[k, at : at + step, :] = x
                total = total + jnp.sum(x.reshape(step // 8, 8, width), axis=0)
            st[r, 0, pl.ds(k, 1), :] = peak
            st[r, 1, pl.ds(k, 1), :] = jnp.sum(total, axis=0, keepdims=True)
            return carry

        lax.fori_loop(begin, end, one, 0)

    def factor(st, f):
        peak = st[0, 0]
        for i in range(1, rows):
            peak = jnp.maximum(peak, st[i, 0])
        total = jnp.zeros_like(peak)
        for i in range(rows):
            total = total + st[i, 1] * jnp.exp(st[i, 0] - peak)
        f[...] = jnp.exp(st[r, 0] - peak) * (1.0 / total)

    for d in range(1, cols):
        slot = lax.rem(c + cols - d, cols)
        q_copy(d, slot).wait_recv()
        q1[slot] = upright(q1t[slot].astype(jnp.float32), lanes)

    def q1_rows(at):
        return q1[at // own : (at + step) // own].reshape(step, q1.shape[2])

    stats(q1_rows, lambda k: t2[k], e1, st1, 0, chunks)
    start_rows(st1, s1_send, s1_recv)

    recv_rows(t1, t_send, t_recv)
    per = width // own

    def t1_rows(k):
        if per == 1:
            return t1[k]
        return jnp.concatenate([t1[k * per + i] for i in range(per)], axis=1)

    def stats_zero(begin, end):
        stats(lambda at: q0[at : at + step, :], t1_rows, e0, st0, begin, end)

    half = (chunks + 1) // 2
    stats_zero(0, half)

    recv_rows(st1, s1_send, s1_recv)
    factor(st1, f1)

    def partial_of(weights, load_prices, block):
        total = jnp.zeros((own, v1_ref.shape[1]), jnp.float32)
        for k in range(chunks):
            total = total + jnp.dot(weights(k, block), load_prices(k), preferred_element_type=jnp.float32)
        return total

    def reduce(weights, load_prices, out, into, send, recv, between):
        def make(d):
            return pltpu.make_async_remote_copy(
                src_ref=out.at[d],
                dst_ref=into.at[d],
                send_sem=send.at[d],
                recv_sem=recv.at[d],
                device_id=(r, lax.rem(c + d, cols)),
                device_id_type=MESH,
            )

        for d in range(1, cols):
            out[d] = partial_of(weights, load_prices, lax.rem(c + d, cols))
            make(d).start()
        total = partial_of(weights, load_prices, c)
        between()
        for d in range(1, cols):
            make(d).wait_recv()
            total = total + into[d]
        return total, lambda: [make(d).wait_send() for d in range(1, cols)]

    def weights_one(k, block):
        return (e1[k, pl.ds(block * own, own), :] * f1[pl.ds(k, 1), :]).astype(jnp.bfloat16)

    def rest_zero():
        stats_zero(half, chunks)
        start_rows(st0, s0_send, s0_recv)

    carried, done1 = reduce(
        weights_one,
        lambda k: terminal_ref[k * width : (k + 1) * width, :],
        out1,
        in1,
        r1_send,
        r1_recv,
        rest_zero,
    )
    value = jnp.where(flags_ref[1:2, :] == 1, jnp.maximum(ex1_ref[...], carried), carried)
    v1_ref[...] = value
    price[r] = value.astype(jnp.bfloat16)
    partner = r + 1 - 2 * lax.rem(r, 2)
    half_rows = rows // 2

    def along(k, slot):
        return pltpu.make_async_remote_copy(
            src_ref=price.at[slot],
            dst_ref=price.at[slot],
            send_sem=p_send.at[k],
            recv_sem=p_recv.at[k],
            device_id=(lax.rem(r + 2 * k, rows), c),
            device_id_type=MESH,
        )

    def across(k, slot):
        return pltpu.make_async_remote_copy(
            src_ref=price.at[slot],
            dst_ref=price.at[slot],
            send_sem=p_send.at[half_rows + k],
            recv_sem=p_recv.at[half_rows + k],
            device_id=(partner, c),
            device_id_type=MESH,
        )

    across(0, r).start()
    for k in range(1, half_rows):
        along(k, r).start()

    recv_rows(st0, s0_send, s0_recv)
    factor(st0, f0)

    def weigh(k, carry):
        for at in range(0, sources, step):
            w0[k, at : at + step, :] = (e0[k, at : at + step, :] * f0[pl.ds(k, 1), :]).astype(jnp.bfloat16)
        return carry

    share = chunks // max(half_rows - 1, 1)
    for k in range(1, half_rows):
        lax.fori_loop((k - 1) * share, chunks if k == half_rows - 1 else k * share, weigh, 0)
        slot = lax.rem(r + rows - 2 * k, rows)
        along(k, slot).wait_recv()
        across(k, slot).start()
    for k in range(half_rows):
        across(k, lax.rem(partner + rows - 2 * k, rows)).wait_recv()

    def price_rows(k):
        return price[k * per : (k + 1) * per].reshape(width, price.shape[2])

    def weights_zero(k, block):
        return w0[k, pl.ds(block * own, own), :]

    carried, done0 = reduce(weights_zero, price_rows, out0, in0, r0_send, r0_recv, lambda: None)
    v0_ref[...] = jnp.where(flags_ref[0:1, :] == 1, jnp.maximum(ex0_ref[...], carried), carried)

    for d in range(1, cols):
        q_copy(d, c).wait_send()
    sent_rows(t1, t_send, t_recv)
    sent_rows(st1, s1_send, s1_recv)
    sent_rows(st0, s0_send, s0_recv)
    for k in range(half_rows):
        across(k, r).wait_send()
        if k:
            along(k, r).wait_send()
    done1()
    done0()


def shards(rows, cols, nodes_zero, nodes_one, nodes_two, precision, drift, terminal, ex1, ex0, flags):
    own, depth = nodes_one.shape
    height = depth + 16
    sources = nodes_zero.shape[0]
    targets = nodes_two.shape[0]
    trades = terminal.shape[1]
    width = max(own, min(TILE, targets))
    chunks = targets // width
    lanes = 128 * (-(-(depth + 3) // 128))
    dma = pltpu.SemaphoreType.DMA
    vmem = pl.BlockSpec(memory_space=pltpu.VMEM)
    out = jax.ShapeDtypeStruct((own, trades), jnp.float32)
    stat = pltpu.VMEM((rows, 2, chunks, width), jnp.float32)
    tall = pltpu.VMEM((chunks, sources, width), jnp.float32)
    few = pltpu.VMEM((chunks, width), jnp.float32)
    parts = pltpu.VMEM((cols, own, trades), jnp.float32)
    return pl.pallas_call(
        functools.partial(body, rows, cols),
        out_shape=(out, out),
        in_specs=[vmem] * 9,
        out_specs=(vmem, vmem),
        scratch_shapes=[
            pltpu.VMEM((cols, height, own), jnp.bfloat16),
            pltpu.VMEM((cols, own, lanes), jnp.bfloat16),
            pltpu.VMEM((rows, lanes, own), jnp.bfloat16),
            pltpu.VMEM((sources, lanes), jnp.bfloat16),
            pltpu.VMEM((chunks, lanes, width), jnp.bfloat16),
            tall,
            tall,
            pltpu.VMEM((chunks, sources, width), jnp.bfloat16),
            stat,
            stat,
            few,
            few,
            pltpu.VMEM((rows, own, trades), jnp.bfloat16),
            parts,
            parts,
            parts,
            parts,
            dma((cols,)),
            dma((cols,)),
            dma((rows,)),
            dma((rows,)),
            dma((rows,)),
            dma((rows,)),
            dma((rows,)),
            dma((rows,)),
            dma((rows,)),
            dma((rows,)),
            dma((cols,)),
            dma((cols,)),
            dma((cols,)),
            dma((cols,)),
        ],
        compiler_params=pltpu.CompilerParams(
            collective_id=0, has_side_effects=True, vmem_limit_bytes=56 * 1024 * 1024
        ),
    )(nodes_zero.T, nodes_one.T, nodes_two.T, precision[None, :], drift[None, :], terminal, ex1, ex0, flags)


def solution(mesh):
    both = P(("row", "col"), None)
    return jax.shard_map(
        functools.partial(shards, mesh.shape["row"], mesh.shape["col"]),
        mesh=mesh,
        in_specs=(P("row", None), both, P("col", None), P(), P(), P("col", None), both, both, P()),
        out_specs=(both, both),
        check_vma=False,
    )
```

time: 61.9 us -> 49.8 us (0.80)
  the two profiles are of different devices: /device:TPU:25 before, /device:TPU:1 now
where the time goes in v2:
time: 49.8 us; the launch traced here: 49.6 us
  Pallas kernels  46.7 us (94%)
  local copies, waits for them, and re-layouts  2.26 us (5%)
  between operations  0.65 us (1%)
    pallas_call x1, Pallas kernels, shards(): pl.pallas_call(functools.partial(body, rows, cols), out_shape=(out, out),...  46.7 us
    unnamed x4, local copies, waits for them, and re-layouts  2.26 us

profile of v2, /device:TPU:1, one launch (start us, length us, event | category | flops | bytes accessed | tf_op | source)
XLA Modules:
  0.0 49.6 jit_solution(18258541195360419352)
XLA Ops:
  0.6 46.7 %shard_map.104 = (f32[256,128]{1,0:T(8,128)}, f32[256,128]{1,0:T(8,128)}) custom-call(f32[64,1024]{1,0:T(8,128)} %bitcast.6, f32[64,256]{1,0:T(8,128)} %bitcast.7, f32[64,2048]{1,0:T(8,128)} %bitcast.5, f32[1,64]{1,0:T(1,128)} %bitcast.8, f32[1,64]{1,0:T(1,128)} %bitcast.9, bf16[2048,128]{1,0:T(8,128)(2,1)} %terminal_ref.1, f32[256,128]{1,0:T(8,128)} %ex1_ref.1, ...), custom_call_target="tpu_custom_call" | custom-call | tf_op jit(solution)/shard_map/pallas_call | solution.py:351
  47.3 0.0 copy-start
  47.4 1.6 %copy.13 = f32[256,128]{1,0:T(8,128)} copy(f32[256,128]{1,0:T(8,128)} %get-tuple-element.4) | data formatting | bytes 262144
  49.0 0.0 copy-done
  49.0 0.7 %copy.14 = f32[256,128]{1,0:T(8,128)} copy(f32[256,128]{1,0:T(8,128)S(1)} %copy-done) | data formatting | bytes 262144
Async XLA Ops:
  47.3 1.6 %copy-start = (f32[256,128]{1,0:T(8,128)S(1)}, f32[256,128]{1,0:T(8,128)}, u32[]{:S(2)}) copy-start(f32[256,128]{1,0:T(8,128)} %get-tuple-element.5) | copy-start | bytes 393220

commit v3 on v2

--- a/solution.py
+++ b/solution.py
@@ -9,6 +9,8 @@
 
 MESH = pl.DeviceIdType.MESH
 TILE = 256
+PARTS = 2
+LIMIT = 62 * 1024 * 1024
 
 
 def column_of(row):
@@ -43,15 +45,26 @@
 def body(
     rows,
     cols,
+    nz_hbm,
+    n1_hbm,
+    n2_hbm,
+    precision_hbm,
+    drift_hbm,
+    terminal_hbm,
+    ex1_hbm,
+    ex0_hbm,
+    flags_hbm,
+    v1_hbm,
+    v0_hbm,
+    precision_ref,
+    drift_ref,
+    flags_ref,
     nz_ref,
     n1_ref,
     n2_ref,
-    precision_ref,
-    drift_ref,
     terminal_ref,
     ex1_ref,
     ex0_ref,
-    flags_ref,
     v1_ref,
     v0_ref,
     q1t,
@@ -85,6 +98,7 @@
     r1_recv,
     r0_send,
     r0_recv,
+    local,
 ):
     r = lax.axis_index("row")
     c = lax.axis_index("col")
@@ -93,18 +107,45 @@
     lanes = q0.shape[1]
     height = q1t.shape[1]
     chunks, _, width = e1.shape
-    precision = column_of(precision_ref[...])
-    drift = column_of(drift_ref[...])
-
     barrier = pltpu.get_barrier_semaphore()
     for d in range(1, rows):
         pl.semaphore_signal(barrier, inc=1, device_id=(lax.rem(r + d, rows), c), device_id_type=MESH)
     for d in range(1, cols):
         pl.semaphore_signal(barrier, inc=1, device_id=(r, lax.rem(c + d, cols)), device_id_type=MESH)
 
+    loads = [
+        pltpu.make_async_copy(a, b, local.at[i])
+        for i, (a, b) in enumerate(
+            [
+                (n1_hbm, n1_ref),
+                (n2_hbm, n2_ref),
+                (nz_hbm, nz_ref),
+                (terminal_hbm, terminal_ref),
+                (ex1_hbm, ex1_ref),
+                (ex0_hbm, ex0_ref),
+                (flags_hbm, flags_ref),
+                (precision_hbm, precision_ref),
+                (drift_hbm, drift_ref),
+            ]
+        )
+    ]
+    for load in loads[7:] + loads[:7]:
+        load.start()
+    loads[7].wait()
+    loads[8].wait()
+    precision = column_of(precision_ref[...])
+    drift = column_of(drift_ref[...])
+    loads[0].wait()
     mine = queries_of(n1_ref[...], precision, drift, height)
     q1t[c] = mine.astype(jnp.bfloat16)
     t1[r, :depth, :] = n1_ref[...].astype(jnp.bfloat16)
+    for i in range(rows):
+        t1[i, depth:, :] = ones_under(lanes - depth, own)
+    loads[1].wait()
+    for k in range(chunks):
+        t2[k, :depth, :] = n2_ref[:, k * width : (k + 1) * width].astype(jnp.bfloat16)
+        t2[k, depth:, :] = ones_under(lanes - depth, width)
+    q1[c] = upright(mine, lanes)
     pl.semaphore_wait(barrier, rows + cols - 2)
 
     def to_rows(buf, send, recv):
@@ -150,14 +191,8 @@
         q_copy(d, c).start()
     start_rows(t1, t_send, t_recv)
 
-    for k in range(chunks):
-        t2[k, :depth, :] = n2_ref[:, k * width : (k + 1) * width].astype(jnp.bfloat16)
-        t2[k, depth:, :] = ones_under(lanes - depth, width)
-    q1[c] = upright(mine, lanes)
+    loads[2].wait()
     q0[...] = upright(queries_of(nz_ref[...], precision, drift, height), lanes)
-    for i in range(rows):
-        t1[i, depth:, :] = ones_under(lanes - depth, own)
-
     step = min(TILE, sources)
 
     def stats(load_queries, load_targets, e, st, begin, end):
@@ -220,78 +255,94 @@
     recv_rows(st1, s1_send, s1_recv)
     factor(st1, f1)
 
-    def partial_of(weights, load_prices, block):
-        total = jnp.zeros((own, v1_ref.shape[1]), jnp.float32)
+    def partial_of(weights, load_prices, first, count):
+        total = jnp.zeros((count, v1_ref.shape[1]), jnp.float32)
         for k in range(chunks):
-            total = total + jnp.dot(weights(k, block), load_prices(k), preferred_element_type=jnp.float32)
+            total = total + jnp.dot(weights(k, first, count), load_prices(k), preferred_element_type=jnp.float32)
         return total
 
-    def reduce(weights, load_prices, out, into, send, recv, between):
-        def make(d):
-            return pltpu.make_async_remote_copy(
-                src_ref=out.at[d],
-                dst_ref=into.at[d],
-                send_sem=send.at[d],
-                recv_sem=recv.at[d],
-                device_id=(r, lax.rem(c + d, cols)),
-                device_id_type=MESH,
-            )
-
+    def carry_copy(out, into, send, recv, d, h, count):
+        return pltpu.make_async_remote_copy(
+            src_ref=out.at[d, pl.ds(h * count, count)],
+            dst_ref=into.at[d, pl.ds(h * count, count)],
+            send_sem=send.at[h * cols + d],
+            recv_sem=recv.at[h * cols + d],
+            device_id=(r, lax.rem(c + d, cols)),
+            device_id_type=MESH,
+        )
+
+    def send_carry(weights, load_prices, out, into, send, recv, parts):
+        count = own // parts
+        for h in range(parts):
+            for d in range(1, cols):
+                first = lax.rem(c + d, cols) * own + h * count
+                part = partial_of(weights, load_prices, first, count)
+                out[d, h * count : (h + 1) * count, :] = part.astype(out.dtype)
+                carry_copy(out, into, send, recv, d, h, count).start()
+        return partial_of(weights, load_prices, c * own, own)
+
+    def take_carry(total, out, into, send, recv, parts, h):
+        count = own // parts
+        piece = slice(h * count, (h + 1) * count)
+        total = total[piece]
         for d in range(1, cols):
-            out[d] = partial_of(weights, load_prices, lax.rem(c + d, cols))
-            make(d).start()
-        total = partial_of(weights, load_prices, c)
-        between()
-        for d in range(1, cols):
-            make(d).wait_recv()
-            total = total + into[d]
-        return total, lambda: [make(d).wait_send() for d in range(1, cols)]
-
-    def weights_one(k, block):
-        return (e1[k, pl.ds(block * own, own), :] * f1[pl.ds(k, 1), :]).astype(jnp.bfloat16)
-
-    def rest_zero():
-        stats_zero(half, chunks)
-        start_rows(st0, s0_send, s0_recv)
-
-    carried, done1 = reduce(
-        weights_one,
-        lambda k: terminal_ref[k * width : (k + 1) * width, :],
-        out1,
-        in1,
-        r1_send,
-        r1_recv,
-        rest_zero,
-    )
-    value = jnp.where(flags_ref[1:2, :] == 1, jnp.maximum(ex1_ref[...], carried), carried)
-    v1_ref[...] = value
-    price[r] = value.astype(jnp.bfloat16)
+            carry_copy(out, into, send, recv, d, h, count).wait_recv()
+            total = total + into[d, piece, :].astype(jnp.float32)
+        return total
+
+    def end_carry(out, into, send, recv, parts):
+        for h in range(parts):
+            for d in range(1, cols):
+                carry_copy(out, into, send, recv, d, h, own // parts).wait_send()
+
+    def weights_one(k, first, count):
+        return (e1[k, pl.ds(first, count), :] * f1[pl.ds(k, 1), :]).astype(jnp.bfloat16)
+
+    loads[3].wait()
+    one = (out1, in1, r1_send, r1_recv, PARTS)
+    held = send_carry(weights_one, lambda k: terminal_ref[k * width : (k + 1) * width, :], *one)
+    stats_zero(half, chunks)
+    start_rows(st0, s0_send, s0_recv)
+    loads[4].wait()
+    loads[6].wait()
     partner = r + 1 - 2 * lax.rem(r, 2)
     half_rows = rows // 2
 
-    def along(k, slot):
+    size = own // PARTS
+
+    def along(k, h, slot):
+        view = price.at[slot, pl.ds(h * size, size)]
         return pltpu.make_async_remote_copy(
-            src_ref=price.at[slot],
-            dst_ref=price.at[slot],
-            send_sem=p_send.at[k],
-            recv_sem=p_recv.at[k],
+            src_ref=view,
+            dst_ref=view,
+            send_sem=p_send.at[h * rows + k],
+            recv_sem=p_recv.at[h * rows + k],
             device_id=(lax.rem(r + 2 * k, rows), c),
             device_id_type=MESH,
         )
 
-    def across(k, slot):
+    def across(k, h, slot):
+        view = price.at[slot, pl.ds(h * size, size)]
         return pltpu.make_async_remote_copy(
-            src_ref=price.at[slot],
-            dst_ref=price.at[slot],
-            send_sem=p_send.at[half_rows + k],
-            recv_sem=p_recv.at[half_rows + k],
+            src_ref=view,
+            dst_ref=view,
+            send_sem=p_send.at[h * rows + half_rows + k],
+            recv_sem=p_recv.at[h * rows + half_rows + k],
             device_id=(partner, c),
             device_id_type=MESH,
         )
 
-    across(0, r).start()
-    for k in range(1, half_rows):
-        along(k, r).start()
+    for h in range(PARTS):
+        piece = slice(h * size, (h + 1) * size)
+        carried = take_carry(held, *one, h)
+        value = jnp.where(flags_ref[1:2, :] == 1, jnp.maximum(ex1_ref[piece, :], carried), carried)
+        v1_ref[piece, :] = value
+        price[r, piece, :] = value.astype(jnp.bfloat16)
+        for k in range(1, half_rows):
+            along(k, h, r).start()
+        across(0, h, r).start()
+    keep_one = pltpu.make_async_copy(v1_ref, v1_hbm, local.at[9])
+    keep_one.start()
 
     recv_rows(st0, s0_send, s0_recv)
     factor(st0, f0)
@@ -301,35 +352,44 @@
             w0[k, at : at + step, :] = (e0[k, at : at + step, :] * f0[pl.ds(k, 1), :]).astype(jnp.bfloat16)
         return carry
 
-    share = chunks // max(half_rows - 1, 1)
-    for k in range(1, half_rows):
-        lax.fori_loop((k - 1) * share, chunks if k == half_rows - 1 else k * share, weigh, 0)
-        slot = lax.rem(r + rows - 2 * k, rows)
-        along(k, slot).wait_recv()
-        across(k, slot).start()
-    for k in range(half_rows):
-        across(k, lax.rem(partner + rows - 2 * k, rows)).wait_recv()
+    lax.fori_loop(0, chunks, weigh, 0)
+    for h in range(PARTS):
+        for k in range(1, half_rows):
+            slot = lax.rem(r + rows - 2 * k, rows)
+            along(k, h, slot).wait_recv()
+            across(k, h, slot).start()
+    for h in range(PARTS):
+        for k in range(half_rows):
+            across(k, h, lax.rem(partner + rows - 2 * k, rows)).wait_recv()
 
     def price_rows(k):
         return price[k * per : (k + 1) * per].reshape(width, price.shape[2])
 
-    def weights_zero(k, block):
-        return w0[k, pl.ds(block * own, own), :]
-
-    carried, done0 = reduce(weights_zero, price_rows, out0, in0, r0_send, r0_recv, lambda: None)
+    def weights_zero(k, first, count):
+        return w0[k, pl.ds(first, count), :]
+
+    zero = (out0, in0, r0_send, r0_recv, 1)
+    held = send_carry(weights_zero, price_rows, *zero)
+    loads[5].wait()
+    carried = take_carry(held, *zero, 0)
     v0_ref[...] = jnp.where(flags_ref[0:1, :] == 1, jnp.maximum(ex0_ref[...], carried), carried)
+    keep_zero = pltpu.make_async_copy(v0_ref, v0_hbm, local.at[10])
+    keep_zero.start()
 
     for d in range(1, cols):
         q_copy(d, c).wait_send()
     sent_rows(t1, t_send, t_recv)
     sent_rows(st1, s1_send, s1_recv)
     sent_rows(st0, s0_send, s0_recv)
-    for k in range(half_rows):
-        across(k, r).wait_send()
-        if k:
-            along(k, r).wait_send()
-    done1()
-    done0()
+    for h in range(PARTS):
+        for k in range(half_rows):
+            across(k, h, r).wait_send()
+            if k:
+                along(k, h, r).wait_send()
+    end_carry(*one)
+    end_carry(*zero)
+    keep_one.wait()
+    keep_zero.wait()
 
 
 def shards(rows, cols, nodes_zero, nodes_one, nodes_two, precision, drift, terminal, ex1, ex0, flags):
@@ -342,18 +402,31 @@
     chunks = targets // width
     lanes = 128 * (-(-(depth + 3) // 128))
     dma = pltpu.SemaphoreType.DMA
-    vmem = pl.BlockSpec(memory_space=pltpu.VMEM)
     out = jax.ShapeDtypeStruct((own, trades), jnp.float32)
     stat = pltpu.VMEM((rows, 2, chunks, width), jnp.float32)
     tall = pltpu.VMEM((chunks, sources, width), jnp.float32)
     few = pltpu.VMEM((chunks, width), jnp.float32)
     parts = pltpu.VMEM((cols, own, trades), jnp.float32)
+    slim = pltpu.VMEM((cols, own, trades), jnp.bfloat16)
+    anywhere = pl.BlockSpec(memory_space=pl.ANY)
+    mine = pltpu.VMEM((own, trades), jnp.float32)
     return pl.pallas_call(
         functools.partial(body, rows, cols),
         out_shape=(out, out),
-        in_specs=[vmem] * 9,
-        out_specs=(vmem, vmem),
+        in_specs=[pl.BlockSpec(memory_space=pltpu.HBM)] * 9,
+        out_specs=(anywhere, anywhere),
         scratch_shapes=[
+            pltpu.VMEM((1, depth), jnp.float32),
+            pltpu.VMEM((1, depth), jnp.float32),
+            pltpu.VMEM((2, trades), jnp.int32),
+            pltpu.VMEM((depth, sources), jnp.float32),
+            pltpu.VMEM((depth, own), jnp.float32),
+            pltpu.VMEM((depth, targets), jnp.float32),
+            pltpu.VMEM((targets, trades), jnp.bfloat16),
+            mine,
+            mine,
+            mine,
+            mine,
             pltpu.VMEM((cols, height, own), jnp.bfloat16),
             pltpu.VMEM((cols, own, lanes), jnp.bfloat16),
             pltpu.VMEM((rows, lanes, own), jnp.bfloat16),
@@ -369,25 +442,17 @@
             pltpu.VMEM((rows, own, trades), jnp.bfloat16),
             parts,
             parts,
-            parts,
-            parts,
-            dma((cols,)),
-            dma((cols,)),
-            dma((rows,)),
-            dma((rows,)),
-            dma((rows,)),
-            dma((rows,)),
-            dma((rows,)),
-            dma((rows,)),
-            dma((rows,)),
-            dma((rows,)),
-            dma((cols,)),
-            dma((cols,)),
-            dma((cols,)),
-            dma((cols,)),
+            slim,
+            slim,
+            *[dma((cols,))] * 2,
+            *[dma((rows,))] * 6,
+            *[dma((PARTS * rows,))] * 2,
+            *[dma((PARTS * cols,))] * 2,
+            *[dma((cols,))] * 2,
+            dma((11,)),
         ],
         compiler_params=pltpu.CompilerParams(
-            collective_id=0, has_side_effects=True, vmem_limit_bytes=56 * 1024 * 1024
+            collective_id=0, has_side_effects=True, vmem_limit_bytes=LIMIT
         ),
     )(nodes_zero.T, nodes_one.T, nodes_two.T, precision[None, :], drift[None, :], terminal, ex1, ex0, flags)
 

time: 49.8 us -> 44.2 us (0.89)
  Pallas kernels: 46.7 us -> 41.1 us
    pallas_call x1, Pallas kernels: 46.7 us -> 41.1 us  [shards(): pl.pallas_call(functools.partial(body, rows, cols), out_shape=(out, out),...]
where the time goes in v3:
time: 44.2 us; the launch traced here: 44 us
  Pallas kernels  41.1 us (93%)
  local copies, waits for them, and re-layouts  2.26 us (5%)
  between operations  0.65 us (1%)
    pallas_call x1, Pallas kernels, shards(): pl.pallas_call(functools.partial(body, rows, cols), out_shape=(out, out),...  41.1 us
    unnamed x4, local copies, waits for them, and re-layouts  2.26 us

profile of v3, /device:TPU:1, one launch (start us, length us, event | category | flops | bytes accessed | tf_op | source)
XLA Modules:
  0.0 44.0 jit_solution(7195178235496706855)
XLA Ops:
  0.6 41.1 %shard_map.104 = (f32[256,128]{1,0:T(8,128)}, f32[256,128]{1,0:T(8,128)}) custom-call(f32[64,1024]{1,0:T(8,128)} %bitcast.6, f32[64,256]{1,0:T(8,128)} %bitcast.7, f32[64,2048]{1,0:T(8,128)} %bitcast.5, f32[1,64]{1,0:T(1,128)} %bitcast.8, f32[1,64]{1,0:T(1,128)} %bitcast.9, bf16[2048,128]{1,0:T(8,128)(2,1)} %terminal_hbm.1, f32[256,128]{1,0:T(8,128)} %ex1_hbm.1, ...), custom_call_target="tpu_custom_call" | custom-call | tf_op jit(solution)/shard_map/pallas_call | solution.py:413
  41.8 0.0 copy-start
  41.8 1.6 %copy.13 = f32[256,128]{1,0:T(8,128)} copy(f32[256,128]{1,0:T(8,128)} %get-tuple-element.4) | data formatting | bytes 262144
  43.4 0.0 copy-done
  43.4 0.7 %copy.14 = f32[256,128]{1,0:T(8,128)} copy(f32[256,128]{1,0:T(8,128)S(1)} %copy-done) | data formatting | bytes 262144
Async XLA Ops:
  41.8 1.6 %copy-start = (f32[256,128]{1,0:T(8,128)S(1)}, f32[256,128]{1,0:T(8,128)}, u32[]{:S(2)}) copy-start(f32[256,128]{1,0:T(8,128)} %get-tuple-element.5) | copy-start | bytes 393220
